TPU v7x, 512 devices: a whole 4x4x16 slice. The times are simulated.
512 devices in a mesh: lat: 64 (over z, y), ord: 2 (over core), orb: 4 (over x).
Axes of the slice: x: 4, y: 4, z: 16, core: 2. Of those that a mesh axis runs over, the one named last changes fastest.
Arguments:
- anomaly: bfloat16 [2, 1024, 4320], P(None, 'lat'), may hold values from -6 to 6
- row_weight: float32 [2, 1024], replicated, may hold values from 0.2 to 1
- panel: bfloat16 [4, 64, 1024, 2, 640], P('orb', None, 'lat', 'ord'), may hold values from -0.125 to 0.125
- order_value: int32 [4, 64], P('orb'), may hold values from 0 to 2159
- deg_first: int32 [4, 64], P('orb', 'lat'), may hold values from 0 to 2190
- sat_rows: bfloat16 [131072, 256], P(('lat', 'ord', 'orb')), may hold values from -0.25 to 0.25
- sat_slot: int32 [131072, 1], P(('lat', 'ord', 'orb')), may hold values from 0 to 255; in each aligned block of 256 rows (0 to 255, 256 to 511, ...) at most 2 rows name the same one
Outputs:
- normals: float32 [4, 64, 2, 640, 2, 640], P('orb', 'lat', 'ord')
- right_side: float32 [4, 64, 2, 2, 640], P('orb', 'lat', None, 'ord')
Inputs may be any that keep to these rules, and one draw needn't show every extreme that they name: `sat_slot`: among the 256 rows of one device no order slot appears more than 2 times.
All inputs are finite; a program needn't handle non-finite values.
Results may differ from a plain program's by a relative error of at most 0.0029.
Values may be sent and summed in bfloat16 or wider, within the bound.
No kernel may reach another device: no remote copies, remote signals or barrier semaphores. Data moves between devices by JAX's collectives and lax.ppermute only.
A program may use at most 64 MiB of HBM per device.

v0:
```python
import math
import jax
import jax.numpy as jnp
from jax import lax
from jax.sharding import PartitionSpec as P

LMAX = 2190


def window_flags(first_degree, order_now, half_count):
    parity_col = (
        jnp.arange(2, dtype=jnp.int32)[:, None]
        + 2 * jnp.arange(half_count, dtype=jnp.int32)[None, :]
    )
    degree = first_degree[:, None, None] + parity_col[None]
    live_flags = (degree <= LMAX).astype(jnp.float32)
    parity = (degree + order_now[:, None, None]) % 2
    return (live_flags, 1.0 - 2.0 * parity.astype(jnp.float32))


def fourier_table(order_row, length):
    sample = jnp.arange(length, dtype=jnp.int32)
    phase_index = sample[:, None] * order_row[None, :] % length
    angle_value = phase_index.astype(jnp.float32) * (2.0 * math.pi / length)
    return jnp.concatenate([jnp.cos(angle_value), jnp.sin(angle_value)], axis=1)


def parity_gram(received):
    sat_width = received.shape[-1]
    sat_block = received.reshape(received.shape[0], -1, sat_width)
    split_block = sat_block.reshape(sat_block.shape[0], sat_block.shape[1], 2, sat_width // 2)
    return jnp.einsum("irpa,irl->pial", split_block, sat_block, preferred_element_type=jnp.float32)


def shards(anomaly, row_weight, panel, order_value, deg_first, sat_rows, sat_slot):
    lat_count = lax.axis_size("lat")
    orb_count = lax.axis_size("orb")
    lat_index = lax.axis_index("lat")
    parity_index = lax.axis_index("ord")
    group_orders = panel.shape[1]
    row_count = panel.shape[2]
    half_count = panel.shape[4]
    lon_count = anomaly.shape[2]
    trig_table = fourier_table(order_value[0], lon_count)
    spectra = jnp.einsum(
        "hrk,kc->hrc", anomaly.astype(jnp.float32), trig_table, precision=lax.Precision.HIGHEST
    ) * math.sqrt(2.0 / lon_count)
    local_weight = lax.dynamic_slice_in_dim(row_weight, lat_index * row_count, row_count, 1)
    north_terms = spectra[0] * local_weight[0][:, None]
    south_terms = spectra[1] * local_weight[1][:, None]
    coefficients = jnp.stack(
        [
            north_terms[:, :group_orders],
            north_terms[:, group_orders:],
            south_terms[:, :group_orders],
            south_terms[:, group_orders:],
        ],
        axis=-1,
    )
    coefficients = jnp.transpose(coefficients, (1, 0, 2))[None].astype(jnp.bfloat16)
    own_order = lax.dynamic_slice_in_dim(order_value[0], lat_index, 1, 0)
    live_pair, sign_pair = window_flags(deg_first[0], own_order, half_count)
    live_own = lax.dynamic_index_in_dim(live_pair[0], parity_index, 0, keepdims=False)
    sign_own = lax.dynamic_index_in_dim(sign_pair[0], parity_index, 0, keepdims=False)
    live_mask = live_own.astype(jnp.bfloat16)
    panel_piece = panel[0, :, :, 0, :]
    coef_piece = coefficients[0]
    summed = lax.psum_scatter(
        jnp.einsum("ori,orc->oci", panel_piece, coef_piece, preferred_element_type=jnp.float32),
        "lat",
        scatter_dimension=0,
        tiled=True,
    )
    products = summed[0] * live_own[None, :]
    arrived_panel = lax.all_to_all(panel, "lat", split_axis=1, concat_axis=2, tiled=True)
    masked_own = arrived_panel[0, 0, :, 0, :] * live_mask[None, :]
    right_cos = products[0] + sign_own * products[2]
    right_sin = products[1] + sign_own * products[3]
    right_side = jnp.stack([right_cos, right_sin], axis=0)[None, None, :, None, :]
    parity_pair = lax.all_gather(masked_own[:, None, :], "ord", axis=1, tiled=True)
    plus_weight = (row_weight[0] + row_weight[1])[:, None, None]
    minus_weight = (row_weight[0] - row_weight[1])[:, None, None]
    plus_panel = (parity_pair.astype(jnp.float32) * plus_weight).astype(jnp.bfloat16)
    minus_panel = (parity_pair.astype(jnp.float32) * minus_weight).astype(jnp.bfloat16)
    full_plus = jnp.einsum(
        "ri,rqj->iqj", masked_own, plus_panel, preferred_element_type=jnp.float32
    )
    full_minus = jnp.einsum(
        "ri,rqj->iqj", masked_own, minus_panel, preferred_element_type=jnp.float32
    )
    same_parity = (jnp.arange(2, dtype=jnp.int32) == parity_index)[None, :, None]
    grid_normal = jnp.where(same_parity, full_plus, full_minus)
    sat_order = sat_slot[:, 0]
    sat_count = sat_order.shape[0]
    sat_width = sat_rows.shape[1]
    half_sat = sat_width // 2
    orders_all = orb_count * group_orders
    slot_cap = max(2, 2 * sat_count // orders_all)
    position = jnp.arange(sat_count, dtype=jnp.int32)
    earlier = (sat_order[:, None] == sat_order[None, :]) & (position[None, :] < position[:, None])
    slot_rank = jnp.sum(earlier, axis=1, dtype=jnp.int32)
    group_id = sat_order // group_orders
    within = sat_order % group_orders
    destination = (group_id * lat_count + within) * slot_cap + slot_rank
    reordered = (
        sat_rows.reshape(sat_count, half_sat, 2).transpose(0, 2, 1).reshape(sat_count, sat_width)
    )
    buffer = (
        jnp.zeros((orb_count * lat_count * slot_cap, sat_width), jnp.bfloat16)
        .at[destination]
        .set(reordered)
    )
    buffer = buffer.reshape(orb_count, lat_count, slot_cap, sat_width)
    partial_value = parity_gram(
        lax.all_to_all(buffer, "lat", split_axis=1, concat_axis=1, tiled=True)
    )
    sat_half = lax.psum_scatter(
        partial_value.reshape(-1, sat_width), ("ord", "orb"), scatter_dimension=0, tiled=True
    )
    sat_block = sat_half.reshape(half_sat, 2, half_sat)
    padded = jnp.pad(sat_block, ((0, half_count - half_sat), (0, 0), (0, half_count - half_sat)))
    normals = grid_normal + padded * (live_own[:, None, None] * live_pair[0][None, :, :])
    return (normals[None, None, None], right_side)


def solution(mesh):
    in_specs = (
        P(None, "lat", None),
        P(),
        P("orb", None, "lat", "ord", None),
        P("orb", None),
        P("orb", "lat"),
        P(("lat", "ord", "orb"), None),
        P(("lat", "ord", "orb"), None),
    )
    out_specs = (P("orb", "lat", "ord", None, None, None), P("orb", "lat", None, "ord", None))
    return jax.shard_map(shards, mesh=mesh, in_specs=in_specs, out_specs=out_specs, check_vma=False)
```

profile of v0, /device:TPU:1, one launch (start us, length us, event | category | flops | bytes accessed | tf_op | source)
XLA Modules:
  0.0 386.9 jit_solution(14121209996420184971)
XLA Ops:
  8.0 0.0 copy-start
  8.0 0.9 convert_reduce_fusion
  8.9 0.7 compare_select_fusion.2
  9.6 1.0 copy.52
  10.7 0.1 reshape.237
  10.7 0.1 copy.54
  10.8 0.0 copy-start.1
  10.9 0.0 copy-start.2
  10.9 1.5 scatter_custom_fusion
  12.4 0.1 reshape.239
  12.5 0.2 copy.55
  12.7 38.5 %all_to_all.14 = bf16[4,64,2,256]{3,2,0,1:T(2,128)(2,1)S(1)} all-to-all(bf16[4,64,2,256]{3,2,0,1:T(2,128)(2,1)S(1)} %copy.55), channel_id=1, replica_groups=mesh['lat'=64,'ord'=2,'orb'=4] {'lat'}, dimensions={1} | all-to-all | bytes 524288 | tf_op jit(solution)/shard_map/all_to_all | solution.py:115
  51.3 7.0 %all-to-all-start = ((bf16[1,64,16,1,640]{4,2,3,0,1:T(8,128)(2,1)}), bf16[1,64,16,1,640]{4,2,3,0,1:T(8,128)(2,1)S(1)}, u32[]{:S(2)}, u32[]{:S(2)}) async-start(bf16[1,64,16,1,640]{4,2,3,0,1:T(8,128)(2,1)} %bitcast), calls=%async_computation | async-start | bytes 2621440 | tf_op jit(solution)/shard_map/all_to_all | solution.py:75
  58.3 0.2 all-reduce.4.cloned.1.call-start
  58.6 0.1 constant_dynamic-slice_fusion.1
  58.7 0.0 copy-done.2
  58.7 8.9 %fusion.16 = (f32[4320,64]{1,0:T(8,128)S(1)}, f32[4320,64]{1,0:T(8,128)S(1)}) fusion(s32[64]{0:T(128)S(1)} %bitcast.98), kind=kLoop, calls=%fused_computation.21 | loop fusion | flops 2488320 | bytes 2212096 | tf_op jit(solution)/shard_map/cos | solution.py:25
  67.6 1.2 fusion.27
  68.8 0.1 fusion.37
  68.9 0.1 slice_bitcast_fusion.3
  69.0 0.1 copy.62
  69.1 2.5 fusion.20
  71.6 0.0 all-reduce.4.cloned.1.call-update
  71.6 0.3 reduce-scatter.2.cloned.1.call-start
  71.9 0.2 copy.56
  72.1 0.2 reshape_reshape.3
  72.3 0.1 reshape.240
  72.4 0.2 copy.58
  72.6 0.3 fusion.48
  72.9 1.0 copy.59
  73.9 0.0 reduce-scatter.2.cloned.1.call-update
  73.9 0.0 all-gather.2.cloned.1.call-start
  74.0 0.6 constant_dynamic-slice_fusion
  75.2 0.7 compare_select_fusion
  75.9 46.8 %all-to-all-done = bf16[1,64,16,1,640]{4,2,3,0,1:T(8,128)(2,1)S(1)} async-done(((bf16[1,64,16,1,640]{4,2,3,0,1:T(8,128)(2,1)}), bf16[1,64,16,1,640]{4,2,3,0,1:T(8,128)(2,1)S(1)}, u32[]{:S(2)}, u32[]{:S(2)}) %all-to-all-start) | async-done | bytes 1310752 | tf_op jit(solution)/shard_map/all_to_all | solution.py:75
  122.8 1.2 broadcast_multiply_fusion
  123.9 0.0 all-gather.2.cloned.1.call-update
  124.0 1.3 dynamic-slice.3
  125.3 212.7 %all-reduce.4.cloned.1.call-done = f32[64,4,640]{2,1,0:T(4,128)} async-done(((f32[64,4,640]{2,1,0:T(4,128)}), f32[64,4,640]{2,1,0:T(4,128)}) %all-reduce.4.cloned.1.call-update) | async-done | bytes 655376
  338.0 1.4 fusion.33
  339.4 0.6 copy.64
  340.0 1.0 copy.60
  341.0 0.1 copy.61
  341.1 0.7 copy.51
  341.7 27.3 %all-gather.2.cloned.1.call-done = bf16[1024,2,640]{2,0,1:T(8,128)(2,1)} async-done(((bf16[1024,1,640]{2,0,1:T(8,128)(2,1)}), bf16[1024,2,640]{2,0,1:T(8,128)(2,1)}) %all-gather.2.cloned.1.call-update) | async-done | bytes 2621456 | tf_op jit(solution)/shard_map/all_gather | solution.py:80
  369.1 3.9 %fusion.2 = f32[640,2,640]{2,0,1:T(8,128)S(1)} fusion(bf16[1024,2,640]{2,0,1:T(8,128)(2,1)} %all-gather.2.cloned.1.call-done, f32[1024]{0:T(1024)S(1)} %bitcast.96, bf16[1024,640]{0,1:T(8,128)(2,1)S(1)} %copy.51, bf16[640]{0:T(1024)(128)(2,1)S(1)} %convert_element_type.57), kind=kOutput, calls=%fused_computation.7 | convolution fusion | flops 1684275200 | bytes 7214336 | tf_op jit(solution)/shard_map/ri,rqj->iqj/dot_general | solution.py:88
  373.0 2.2 add_bitcast_fusion
  375.2 4.2 %copy.63 = f32[1,1,1,640,2,640]{5,4,3,2,1,0:T(2,128)} copy(f32[1,1,1,640,2,640]{5,3,4,2,1,0:T(8,128)S(1)} %add_bitcast_fusion) | data formatting | bytes 6553600
  (16 shorter events, 0.1 us)
Async XLA Ops:
  8.0 59.6 %copy-start = (bf16[2,16,4320]{2,1,0:T(8,128)(2,1)S(1)}, bf16[2,16,4320]{2,1,0:T(8,128)(2,1)}, u32[]{:S(2)}) copy-start(bf16[2,16,4320]{2,1,0:T(8,128)(2,1)} %param.7) | copy-start | bytes 829444
  10.8 47.7 %copy-start.1 = (f32[2,1024]{1,0:T(2,128)S(1)}, f32[2,1024]{1,0:T(2,128)}, u32[]{:S(2)}) copy-start(f32[2,1024]{1,0:T(2,128)} %param.8) | copy-start | bytes 24580
  10.9 47.8 %copy-start.2 = (s32[1,64]{1,0:T(1,128)S(1)}, s32[1,64]{1,0:T(1,128)}, u32[]{:S(2)}) copy-start(s32[1,64]{1,0:T(1,128)} %param.10) | copy-start | bytes 772
  51.3 71.5 %all-to-all-start = ((bf16[1,64,16,1,640]{4,2,3,0,1:T(8,128)(2,1)}), bf16[1,64,16,1,640]{4,2,3,0,1:T(8,128)(2,1)S(1)}, u32[]{:S(2)}, u32[]{:S(2)}) async-start(bf16[1,64,16,1,640]{4,2,3,0,1:T(8,128)(2,1)} %bitcast), calls=%async_computation | async-start | bytes 2621440 | tf_op jit(solution)/shard_map/all_to_all | solution.py:75
  58.3 279.6 %all-reduce.4.cloned.1.call-start = ((), (), s32[]{:S(2)}) async-start(), calls=%async_computation.5 | async-start | bytes 1310720
  71.6 268.3 %reduce-scatter.2.cloned.1.call-start = ((), (), s32[]{:S(2)}) async-start(), calls=%async_computation.4 | async-start | bytes 1179648 | tf_op jit(solution)/shard_map/reduce_scatter | solution.py:117
  73.9 295.1 %all-gather.2.cloned.1.call-start = ((), (), s32[]{:S(2)}) async-start(), calls=%async_computation.3 | async-start | bytes 3932160 | tf_op jit(solution)/shard_map/all_gather | solution.py:80
  369.1 3.9 %copy-start.3 = (bf16[1024,2,640]{2,0,1:T(8,128)(2,1)S(1)}, bf16[1024,2,640]{2,0,1:T(8,128)(2,1)}, u32[]{:S(2)}) copy-start(bf16[1024,2,640]{2,0,1:T(8,128)(2,1)} %all-gather.2.cloned.1.call-done) | copy-start | bytes 7864324
Sparse Core Ops, SparseCore 0:
  71.7 266.1 all-reduce.3
  340.6 28.3 all-gather.1
Sparse Core Ops, SparseCore 1:
  74.9 44.1 reduce-scatter.1
where the time goes:
time: 387 us
  waiting for transfers between devices  287 us (74%)
  blocking collectives  38.5 us (10%)
  between operations  16.4 us (4%)
  other arithmetic  13.9 us (4%)
  local copies, waits for them, and re-layouts  13.4 us (3%)
  matrix products  10.1 us (3%)
  starting transfers between devices  7.58 us (2%)
    unnamed x4, waiting for transfers between devices  213 us
    all_to_all x1, waiting for transfers between devices, shards(): lax.all_to_all(panel, 'lat', split_axis=1, concat_axis=2, tiled=True)  46.8 us
    all_to_all x1, blocking collectives, shards(): lax.all_to_all(buffer, 'lat', split_axis=1, concat_axis=1, tiled=True)  38.5 us
    all_gather x1, waiting for transfers between devices, shards(): lax.all_gather(masked_own[:, None, :], 'ord', axis=1, tiled=True)  27.3 us
    cos x1, other arithmetic, fourier_table(): return jnp.concatenate([jnp.cos(angle_value), jnp.sin(angle_value)], axis=1)  8.9 us
  transfers between devices with their start and end apart: 4, of which 3 were waited for; matrix products, arithmetic and copies ran while one was open for 6% of the time, Pallas kernels for 0%

commit v1 on v0

--- a/solution.py
+++ b/solution.py
@@ -5,6 +5,14 @@
 from jax.sharding import PartitionSpec as P
 
 LMAX = 2190
+
+
+def tiled_gather(array, axis, dim):
+    devices = lax.axis_size(axis)
+    repeats = [devices if d == dim else 1 for d in range(array.ndim)]
+    return lax.all_to_all(
+        jnp.tile(array, repeats), axis, split_axis=dim, concat_axis=dim, tiled=True
+    )
 
 
 def window_flags(first_degree, order_now, half_count):
@@ -77,7 +85,7 @@
     right_cos = products[0] + sign_own * products[2]
     right_sin = products[1] + sign_own * products[3]
     right_side = jnp.stack([right_cos, right_sin], axis=0)[None, None, :, None, :]
-    parity_pair = lax.all_gather(masked_own[:, None, :], "ord", axis=1, tiled=True)
+    parity_pair = tiled_gather(masked_own[:, None, :], "ord", 1)
     plus_weight = (row_weight[0] + row_weight[1])[:, None, None]
     minus_weight = (row_weight[0] - row_weight[1])[:, None, None]
     plus_panel = (parity_pair.astype(jnp.float32) * plus_weight).astype(jnp.bfloat16)

time: 387 us -> 376 us (0.972)
  blocking collectives: 38.5 us -> 16.2 us
  starting transfers between devices: 7.58 us -> 26.8 us
  waiting for transfers between devices: 287 us -> 280 us
    unnamed x4 -> x3, waiting for transfers between devices: 213 us -> 261 us
    all_to_all x1, waiting for transfers between devices: 46.8 us -> 0.01 us  [shards(): lax.all_to_all(panel, 'lat', split_axis=1, concat_axis=2, tiled=True)]
    all_gather x1 -> x0, waiting for transfers between devices: 27.3 us -> none  [shards(): lax.all_gather(masked_own[:, None, :], 'ord', axis=1, tiled=True)]
    all_to_all x1, blocking collectives: 38.5 us -> 16.2 us  [tiled_gather(): lax.all_to_all(jnp.tile(array, repeats), axis, split_axis=dim, concat_axi...]
    all_to_all x0 -> x1, waiting for transfers between devices: none -> 19.4 us  [shards(): lax.all_to_all(buffer, 'lat', split_axis=1, concat_axis=1, tiled=True)]
    all_to_all x0 -> x1, starting transfers between devices: none -> 19.3 us  [shards(): lax.all_to_all(buffer, 'lat', split_axis=1, concat_axis=1, tiled=True)]
  transfers between devices with their start and end apart: 4 -> 4, of which waited for: 3 -> 2; matrix products, arithmetic and copies ran while one was open for 6% -> 5% of each run, Pallas kernels for 0% -> 0%
where the time goes in v1:
time: 376 us; the launch traced here: 375 us
  waiting for transfers between devices  280 us (74%)
  starting transfers between devices  26.8 us (7%)
  between operations  16.4 us (4%)
  blocking collectives  16.2 us (4%)
  local copies, waits for them, and re-layouts  15 us (4%)
  other arithmetic  12.9 us (3%)
  matrix products  8.12 us (2%)
    unnamed x3, waiting for transfers between devices  261 us
    all_to_all x1, waiting for transfers between devices, shards(): lax.all_to_all(buffer, 'lat', split_axis=1, concat_axis=1, tiled=True)  19.4 us
    all_to_all x1, starting transfers between devices, shards(): lax.all_to_all(buffer, 'lat', split_axis=1, concat_axis=1, tiled=True)  19.3 us
    all_to_all x1, blocking collectives, tiled_gather(): lax.all_to_all(jnp.tile(array, repeats), axis, split_axis=dim, concat_axi...  16.2 us
    cos x1, other arithmetic, fourier_table(): return jnp.concatenate([jnp.cos(angle_value), jnp.sin(angle_value)], axis=1)  8.9 us
  transfers between devices with their start and end apart: 4, of which 2 were waited for; matrix products, arithmetic and copies ran while one was open for 5% of the time, Pallas kernels for 0%

profile of v1, /device:TPU:1, one launch (start us, length us, event | category | flops | bytes accessed | tf_op | source)
XLA Modules:
  0.0 375.4 jit_solution(11321519771747188495)
XLA Ops:
  8.0 0.0 copy-start
  8.0 0.0 copy-start.1
  8.0 0.9 convert_reduce_fusion
  9.0 0.7 compare_select_fusion.2
  9.7 1.0 copy.57
  10.7 0.1 reshape.230
  10.8 0.1 copy.59
  10.9 0.0 copy-start.2
  10.9 1.5 scatter_custom_fusion
  12.4 0.1 reshape.232
  12.5 0.9 copy.60
  13.4 19.3 %all-to-all-start.2 = ((bf16[4,64,2,256]{3,2,0,1:T(2,128)(2,1)}), bf16[4,64,2,256]{3,2,0,1:T(2,128)(2,1)S(1)}, u32[]{:S(2)}, u32[]{:S(2)}) async-start(bf16[4,64,2,256]{3,2,0,1:T(2,128)(2,1)} %copy.60), calls=%async_computation.2 | async-start | bytes 524288 | tf_op jit(solution)/shard_map/all_to_all | solution.py:123
  32.7 0.1 constant_dynamic-slice_fusion.1
  32.8 19.4 %all-to-all-done.2 = bf16[4,64,2,256]{3,2,0,1:T(2,128)(2,1)S(1)} async-done(((bf16[4,64,2,256]{3,2,0,1:T(2,128)(2,1)}), bf16[4,64,2,256]{3,2,0,1:T(2,128)(2,1)S(1)}, u32[]{:S(2)}, u32[]{:S(2)}) %all-to-all-start.2) | async-done | bytes 262176 | tf_op jit(solution)/shard_map/all_to_all | solution.py:123
  52.2 7.0 %all-to-all-start = ((bf16[1,64,16,1,640]{4,2,3,0,1:T(8,128)(2,1)}), bf16[1,64,16,1,640]{4,2,3,0,1:T(8,128)(2,1)S(1)}, u32[]{:S(2)}, u32[]{:S(2)}) async-start(bf16[1,64,16,1,640]{4,2,3,0,1:T(8,128)(2,1)} %bitcast), calls=%async_computation | async-start | bytes 2621440 | tf_op jit(solution)/shard_map/all_to_all | solution.py:83
  59.2 0.2 all-reduce.4.cloned.1.call-start
  59.5 8.9 %fusion.16 = (f32[4320,64]{1,0:T(8,128)S(1)}, f32[4320,64]{1,0:T(8,128)S(1)}) fusion(s32[64]{0:T(128)S(1)} %bitcast.96), kind=kLoop, calls=%fused_computation.21 | loop fusion | flops 2488320 | bytes 2212096 | tf_op jit(solution)/shard_map/cos | solution.py:33
  68.4 1.2 fusion.25
  69.6 0.1 fusion.33
  69.7 0.1 slice_bitcast_fusion.3
  69.8 0.1 copy.67
  69.9 2.5 fusion.20
  72.4 0.0 all-reduce.4.cloned.1.call-update
  72.4 0.3 reduce-scatter.2.cloned.1.call-start
  72.7 0.2 copy.61
  72.9 0.2 reshape_reshape.3
  73.1 0.1 reshape.233
  73.2 0.2 copy.63
  73.4 0.3 fusion.44
  73.6 1.0 copy.64
  74.7 0.0 reduce-scatter.2.cloned.1.call-update
  74.7 0.6 constant_dynamic-slice_fusion
  76.0 0.7 compare_select_fusion
  76.7 1.3 dynamic-slice.3
  78.0 260.6 %all-reduce.4.cloned.1.call-done = f32[64,4,640]{2,1,0:T(4,128)} async-done(((f32[64,4,640]{2,1,0:T(4,128)}), f32[64,4,640]{2,1,0:T(4,128)}) %all-reduce.4.cloned.1.call-update) | async-done | bytes 655376
  338.5 1.4 fusion.29
  339.9 0.6 copy.69
  340.5 1.0 copy.65
  341.5 0.1 copy.66
  341.7 0.0 all-to-all-done
  341.7 0.7 copy.55
  342.3 0.2 broadcast_multiply_fusion
  342.5 0.7 copy.56
  343.2 0.2 tile.2
  343.4 16.2 %all_to_all.19 = bf16[1024,2,640]{2,0,1:T(8,128)(2,1)S(1)} all-to-all(bf16[1024,2,640]{2,0,1:T(8,128)(2,1)S(1)} %tile.2), channel_id=1, replica_groups=mesh['lat'=64,'ord'=2,'orb'=4] {'ord'}, dimensions={1} | all-to-all | bytes 5242880 | tf_op jit(solution)/shard_map/all_to_all | solution.py:13
  359.6 2.0 fusion.2
  361.7 2.1 add_bitcast_fusion
  363.8 4.2 %copy.68 = f32[1,1,1,640,2,640]{5,4,3,2,1,0:T(2,128)} copy(f32[1,1,1,640,2,640]{5,3,4,2,1,0:T(8,128)S(1)} %add_bitcast_fusion) | data formatting | bytes 6553600
  (15 shorter events, 0.1 us)
Async XLA Ops:
  8.0 60.4 %copy-start = (bf16[2,16,4320]{2,1,0:T(8,128)(2,1)S(1)}, bf16[2,16,4320]{2,1,0:T(8,128)(2,1)}, u32[]{:S(2)}) copy-start(bf16[2,16,4320]{2,1,0:T(8,128)(2,1)} %param.7) | copy-start | bytes 829444
  8.0 24.7 %copy-start.1 = (f32[2,1024]{1,0:T(2,128)S(1)}, f32[2,1024]{1,0:T(2,128)}, u32[]{:S(2)}) copy-start(f32[2,1024]{1,0:T(2,128)} %param.8) | copy-start | bytes 24580
  10.9 48.6 %copy-start.2 = (s32[1,64]{1,0:T(1,128)S(1)}, s32[1,64]{1,0:T(1,128)}, u32[]{:S(2)}) copy-start(s32[1,64]{1,0:T(1,128)} %param.10) | copy-start | bytes 772
  13.4 38.8 %all-to-all-start.2 = ((bf16[4,64,2,256]{3,2,0,1:T(2,128)(2,1)}), bf16[4,64,2,256]{3,2,0,1:T(2,128)(2,1)S(1)}, u32[]{:S(2)}, u32[]{:S(2)}) async-start(bf16[4,64,2,256]{3,2,0,1:T(2,128)(2,1)} %copy.60), calls=%async_computation.2 | async-start | bytes 524288 | tf_op jit(solution)/shard_map/all_to_all | solution.py:123
  52.2 289.5 %all-to-all-start = ((bf16[1,64,16,1,640]{4,2,3,0,1:T(8,128)(2,1)}), bf16[1,64,16,1,640]{4,2,3,0,1:T(8,128)(2,1)S(1)}, u32[]{:S(2)}, u32[]{:S(2)}) async-start(bf16[1,64,16,1,640]{4,2,3,0,1:T(8,128)(2,1)} %bitcast), calls=%async_computation | async-start | bytes 2621440 | tf_op jit(solution)/shard_map/all_to_all | solution.py:83
  59.2 279.3 %all-reduce.4.cloned.1.call-start = ((), (), s32[]{:S(2)}) async-start(), calls=%async_computation.5 | async-start | bytes 1310720
  72.4 268.1 %reduce-scatter.2.cloned.1.call-start = ((), (), s32[]{:S(2)}) async-start(), calls=%async_computation.4 | async-start | bytes 1179648 | tf_op jit(solution)/shard_map/reduce_scatter | solution.py:125
Sparse Core Ops, SparseCore 0:
  72.5 265.9 all-reduce.3
Sparse Core Ops, SparseCore 1:
  76.3 44.1 reduce-scatter.1
